TPU v7x, 32 devices: a whole 2x2x4 slice. The times are simulated.
32 devices in a mesh: dp: 8 (over z, core), tensor: 4 (over y, x).
Axes of the slice: x: 2, y: 2, z: 4, core: 2. Of those that a mesh axis runs over, the one named last changes fastest.
Arguments:
- tokens: bfloat16 [8192, 2048], P('dp'), may hold values from -6 to 6
- cotangent: bfloat16 [8192, 2048], P('dp'), may hold values from -6 to 6
- seq_lengths: int32 [4], replicated, may hold values from 1536 to 2048, as said below
- slot_seq: int32 [4], replicated, may hold values from 0 to 3, each once
- w_query: float32 [2048, 2048], P('dp', 'tensor'), may hold values from -0.125 to 0.125
- w_key: float32 [2048, 2048], P('dp', 'tensor'), may hold values from -0.125 to 0.125
- w_value: float32 [2048, 2048], P('dp', 'tensor'), may hold values from -0.125 to 0.125
- b_query: float32 [2048], P('tensor'), may hold values from -3 to 3
- b_value: float32 [2048], P('tensor'), may hold values from -3 to 3
- w_out: float32 [2048, 2048], P('tensor', 'dp'), may hold values from -4 to 4
- b_out: float32 [2048], replicated, may hold values from -3 to 3
- ln1_gain: float32 [2048], replicated, may hold values from 0.5 to 1.5
- ln1_bias: float32 [2048], replicated, may hold values from -3 to 3
- w_inner: float32 [2048, 8192], P('dp', 'tensor'), may hold values from -0.125 to 0.125
- b_inner: float32 [8192], P('tensor'), may hold values from -3 to 3
- w_outer: float32 [8192, 2048], P('tensor', 'dp'), may hold values from -0.0625 to 0.0625
- b_outer: float32 [2048], replicated, may hold values from -3 to 3
- ln2_gain: float32 [2048], replicated, may hold values from 0.5 to 1.5
- ln2_bias: float32 [2048], replicated, may hold values from -3 to 3
Outputs:
- output: float32 [8192, 2048], P('dp')
- grad_tokens: float32 [8192, 2048], P('dp')
- grad_w_query: float32 [2048, 2048], P('dp', 'tensor')
- grad_w_key: float32 [2048, 2048], P('dp', 'tensor')
- grad_w_value: float32 [2048, 2048], P('dp', 'tensor')
- grad_b_query: float32 [2048], P('tensor')
- grad_b_value: float32 [2048], P('tensor')
- grad_w_out: float32 [2048, 2048], P('tensor', 'dp')
- grad_b_out: float32 [2048], replicated
- grad_ln1_gain: float32 [2048], replicated
- grad_ln1_bias: float32 [2048], replicated
- grad_w_inner: float32 [2048, 8192], P('dp', 'tensor')
- grad_b_inner: float32 [8192], P('tensor')
- grad_w_outer: float32 [8192, 2048], P('tensor', 'dp')
- grad_b_outer: float32 [2048], replicated
- grad_ln2_gain: float32 [2048], replicated
- grad_ln2_bias: float32 [2048], replicated
Inputs may be any that keep to these rules, and one draw needn't show every extreme that they name: `seq_lengths`: each sequence's valid tokens; some sequence has exactly 2048 and some exactly 1536. `slot_seq`: each sequence stands in exactly one slot.
All inputs are finite; a program needn't handle non-finite values.
Results may differ from a plain program's by a relative error of at most 0.019.
Values may be sent and summed in bfloat16 or wider, within the bound.
No kernel may reach another device: no remote copies, remote signals or barrier semaphores. Data moves between devices by JAX's collectives and lax.ppermute only.
A program may use at most 256 MiB of HBM per device.

v0:
```python
import jax
import jax.numpy as jnp
from jax import lax
from jax.sharding import PartitionSpec as P

HEAD_DIM = 128
SLOT = 2048
norm_eps = 1e-12


def passed_along(value, axis, steps):
    count = lax.axis_size(axis)
    leading, last = (max(0, -steps), min(count, count - steps))
    return lax.ppermute(value, axis, [(source, source + steps) for source in range(leading, last)])


def layer_norm(resid, gain, shift):
    center = resid - jnp.mean(resid, axis=-1, keepdims=True)
    spread = jnp.mean(center * center, axis=-1, keepdims=True)
    return center * lax.rsqrt(spread + norm_eps) * gain + shift


def gelu_tanh(inner):
    return 0.5 * inner * (1.0 + jnp.tanh(0.7978845608 * (inner + 0.044715 * inner * inner * inner)))


def mat_bf(left, right):
    return jnp.dot(left, right, preferred_element_type=jnp.float32)


def tensor_total(part):
    return lax.psum(part, "tensor")


def on_device(
    tokens,
    cotangent,
    seq_lengths,
    slot_seq,
    w_query,
    w_key,
    w_value,
    b_query,
    b_value,
    w_out,
    b_out,
    ln1_gain,
    ln1_bias,
    w_inner,
    b_inner,
    w_outer,
    b_outer,
    ln2_gain,
    ln2_bias,
):
    tok_rows = tokens.shape[0]
    shard_count = SLOT // tok_rows
    width_here = w_query.shape[1]
    heads_here = width_here // HEAD_DIM
    score_scale = HEAD_DIM ** (-0.5)
    block_rows = min(512, tok_rows)
    block_count = tok_rows // block_rows
    dp_place = lax.axis_index("dp")
    my_slot = dp_place // shard_count
    my_spot = dp_place % shard_count
    slot_ids = jnp.arange(slot_seq.shape[0])
    slot_lengths = jnp.sum(
        jnp.where(slot_seq[:, None] == slot_ids[None, :], seq_lengths[None, :], 0), axis=1
    )
    my_length = jnp.sum(jnp.where(slot_ids == my_slot, slot_lengths, 0))
    row_live = (my_spot * tok_rows + jnp.arange(tok_rows) < my_length).astype(jnp.float32)
    key_live = jnp.arange(SLOT) < my_length
    spot_ids = jnp.arange(shard_count)
    offset_list = [step_by for step_by in range(1 - shard_count, shard_count) if step_by != 0]
    own_hit = (spot_ids == my_spot)[:, None, None]
    tokens_wide = tokens.astype(jnp.float32)
    cot_wide = cotangent.astype(jnp.float32)
    full_query, full_key, full_value, full_out = (
        lax.all_gather(w_query.astype(jnp.bfloat16), "dp", axis=0, tiled=True),
        lax.all_gather(w_key.astype(jnp.bfloat16), "dp", axis=0, tiled=True),
        lax.all_gather(w_value.astype(jnp.bfloat16), "dp", axis=0, tiled=True),
        lax.all_gather(w_out.astype(jnp.bfloat16), "dp", axis=1, tiled=True),
    )
    query_rows = (mat_bf(tokens, full_query) + b_query).astype(jnp.bfloat16)
    key_rows = mat_bf(tokens, full_key).astype(jnp.bfloat16)
    value_rows = (mat_bf(tokens, full_value) + b_value).astype(jnp.bfloat16)
    empty_slab = jnp.zeros((shard_count, tok_rows, width_here), jnp.bfloat16)
    key_slab = jnp.where(own_hit, key_rows[None], empty_slab)
    value_slab = jnp.where(own_hit, value_rows[None], empty_slab)
    for step_by in offset_list:
        far_key, far_value = passed_along((key_rows, value_rows), "dp", step_by)
        far_hit = (spot_ids == my_spot - step_by)[:, None, None]
        key_slab = jnp.where(far_hit, far_key[None], key_slab)
        value_slab = jnp.where(far_hit, far_value[None], value_slab)
    slot_keys = key_slab.reshape(SLOT, heads_here, HEAD_DIM)
    slot_values = value_slab.reshape(SLOT, heads_here, HEAD_DIM)
    query_blocks = query_rows.reshape(block_count, block_rows, heads_here, HEAD_DIM)

    def score_block(query_part):
        scores = (
            jnp.einsum("qhd,khd->hqk", query_part, slot_keys, preferred_element_type=jnp.float32)
            * score_scale
        )
        return jnp.where(key_live[None, None, :], scores, -1e30)

    def forward_block(query_part):
        scores = score_block(query_part)
        top = jnp.max(scores, axis=-1, keepdims=True)
        expd = jnp.exp(scores - top)
        total = jnp.sum(expd, axis=-1, keepdims=True)
        probs = expd / total
        mixed = jnp.einsum(
            "hqk,khd->qhd",
            probs.astype(jnp.bfloat16),
            slot_values,
            preferred_element_type=jnp.float32,
        )
        return (mixed, top + jnp.log(total))

    mixed_blocks, lse_blocks = lax.map(forward_block, query_blocks)
    heads_rows = mixed_blocks.reshape(tok_rows, width_here).astype(jnp.bfloat16)
    attn_part = mat_bf(heads_rows, full_out)
    attn = tensor_total(attn_part) + b_out
    resid_one = tokens_wide + attn
    hidden, norm_one_back = jax.vjp(layer_norm, resid_one, ln1_gain, ln1_bias)
    hidden_low = hidden.astype(jnp.bfloat16)
    full_inner, full_outer = (
        lax.all_gather(w_inner.astype(jnp.bfloat16), "dp", axis=0, tiled=True),
        lax.all_gather(w_outer.astype(jnp.bfloat16), "dp", axis=1, tiled=True),
    )
    inner = mat_bf(hidden_low, full_inner) + b_inner
    act_low = gelu_tanh(inner).astype(jnp.bfloat16)
    outer_part = mat_bf(act_low, full_outer)
    outer = tensor_total(outer_part) + b_outer
    output, norm_two_back = jax.vjp(layer_norm, hidden + outer, ln2_gain, ln2_bias)
    grad_out = cot_wide * row_live[:, None]
    grad_two, grad_ln2_gain, grad_ln2_bias = norm_two_back(grad_out)
    back_inner, back_outer = (
        lax.all_gather(w_inner.astype(jnp.bfloat16), "dp", axis=0, tiled=True),
        lax.all_gather(w_outer.astype(jnp.bfloat16), "dp", axis=1, tiled=True),
    )
    outer_low = grad_two.astype(jnp.bfloat16)
    grad_b_outer = jnp.sum(grad_two, axis=0)
    grad_w_outer = jnp.einsum("tf,td->fd", act_low, outer_low, preferred_element_type=jnp.float32)
    grad_act = jnp.einsum("td,fd->tf", outer_low, back_outer, preferred_element_type=jnp.float32)
    gelu_value, gelu_back = jax.vjp(gelu_tanh, inner)
    inner_low = gelu_back(grad_act)[0].astype(jnp.bfloat16)
    grad_b_inner = jnp.sum(inner_low.astype(jnp.float32), axis=0)
    grad_w_inner = jnp.einsum(
        "td,tf->df", hidden_low, inner_low, preferred_element_type=jnp.float32
    )
    grad_w_inner, grad_w_outer = (
        lax.psum_scatter(
            grad_w_inner.astype(jnp.bfloat16), "dp", scatter_dimension=0, tiled=True
        ).astype(jnp.float32),
        lax.psum_scatter(
            grad_w_outer.astype(jnp.bfloat16), "dp", scatter_dimension=1, tiled=True
        ).astype(jnp.float32),
    )
    hidden_part = jnp.einsum("tf,df->td", inner_low, back_inner, preferred_element_type=jnp.float32)
    grad_hidden = grad_two + tensor_total(hidden_part)
    grad_one, grad_ln1_gain, grad_ln1_bias = norm_one_back(grad_hidden)
    attn_low = grad_one.astype(jnp.bfloat16)
    grad_b_out = jnp.sum(grad_one, axis=0)
    back_query, back_key, back_value, back_out = (
        lax.all_gather(w_query.astype(jnp.bfloat16), "dp", axis=0, tiled=True),
        lax.all_gather(w_key.astype(jnp.bfloat16), "dp", axis=0, tiled=True),
        lax.all_gather(w_value.astype(jnp.bfloat16), "dp", axis=0, tiled=True),
        lax.all_gather(w_out.astype(jnp.bfloat16), "dp", axis=1, tiled=True),
    )
    grad_w_out = jnp.einsum("tc,td->cd", heads_rows, attn_low, preferred_element_type=jnp.float32)
    mixed_low = jnp.einsum(
        "td,cd->tc", attn_low, back_out, preferred_element_type=jnp.float32
    ).astype(jnp.bfloat16)
    grad_blocks = mixed_low.reshape(block_count, block_rows, heads_here, HEAD_DIM)

    def backward_block(carry, inputs):
        key_sum, value_sum = carry
        query_part, grad_part, lse_part = inputs
        probs = jnp.exp(score_block(query_part) - lse_part)
        grad_probs = jnp.einsum(
            "qhd,khd->hqk", grad_part, slot_values, preferred_element_type=jnp.float32
        )
        inner_sum = jnp.sum(probs * grad_probs, axis=-1, keepdims=True)
        score_low = (probs * (grad_probs - inner_sum)).astype(jnp.bfloat16)
        grad_query = (
            jnp.einsum("hqk,khd->qhd", score_low, slot_keys, preferred_element_type=jnp.float32)
            * score_scale
        )
        key_sum = (
            key_sum
            + jnp.einsum("hqk,qhd->khd", score_low, query_part, preferred_element_type=jnp.float32)
            * score_scale
        )
        value_sum = value_sum + jnp.einsum(
            "hqk,qhd->khd",
            probs.astype(jnp.bfloat16),
            grad_part,
            preferred_element_type=jnp.float32,
        )
        return ((key_sum, value_sum), grad_query)

    zero_slab = jnp.zeros((SLOT, heads_here, HEAD_DIM), jnp.float32)
    (key_sum, value_sum), grad_query_blocks = lax.scan(
        backward_block, (zero_slab, zero_slab), (query_blocks, grad_blocks, lse_blocks)
    )
    key_grad_slab = key_sum.reshape(shard_count, tok_rows, width_here)
    value_grad_slab = value_sum.reshape(shard_count, tok_rows, width_here)
    grad_key = jnp.sum(jnp.where(own_hit, key_grad_slab, 0.0), axis=0)
    grad_value = jnp.sum(jnp.where(own_hit, value_grad_slab, 0.0), axis=0)
    for step_by in offset_list:
        far_hit = (spot_ids == my_spot - step_by)[:, None, None]
        send_key = jnp.sum(jnp.where(far_hit, key_grad_slab, 0.0), axis=0)
        send_value = jnp.sum(jnp.where(far_hit, value_grad_slab, 0.0), axis=0)
        back_key_rows, back_value_rows = (
            passed_along(send_key.astype(jnp.bfloat16), "dp", -step_by).astype(send_key.dtype),
            passed_along(send_value.astype(jnp.bfloat16), "dp", -step_by).astype(send_value.dtype),
        )
        grad_key = grad_key + back_key_rows
        grad_value = grad_value + back_value_rows
    query_low = grad_query_blocks.reshape(tok_rows, width_here).astype(jnp.bfloat16)
    key_low = grad_key.astype(jnp.bfloat16)
    value_low = grad_value.astype(jnp.bfloat16)
    grad_w_query = jnp.einsum("td,tc->dc", tokens, query_low, preferred_element_type=jnp.float32)
    grad_w_key = jnp.einsum("td,tc->dc", tokens, key_low, preferred_element_type=jnp.float32)
    grad_w_value = jnp.einsum("td,tc->dc", tokens, value_low, preferred_element_type=jnp.float32)
    grad_b_query = jnp.sum(query_low.astype(jnp.float32), axis=0)
    grad_b_value = jnp.sum(value_low.astype(jnp.float32), axis=0)
    input_part = jnp.einsum("tc,dc->td", query_low, back_query, preferred_element_type=jnp.float32)
    input_part = input_part + jnp.einsum(
        "tc,dc->td", key_low, back_key, preferred_element_type=jnp.float32
    )
    input_part = input_part + jnp.einsum(
        "tc,dc->td", value_low, back_value, preferred_element_type=jnp.float32
    )
    grad_tokens = grad_one + tensor_total(input_part)
    grad_w_query, grad_w_key, grad_w_value, grad_w_out = (
        lax.psum_scatter(
            grad_w_query.astype(jnp.bfloat16), "dp", scatter_dimension=0, tiled=True
        ).astype(jnp.float32),
        lax.psum_scatter(
            grad_w_key.astype(jnp.bfloat16), "dp", scatter_dimension=0, tiled=True
        ).astype(jnp.float32),
        lax.psum_scatter(
            grad_w_value.astype(jnp.bfloat16), "dp", scatter_dimension=0, tiled=True
        ).astype(jnp.float32),
        lax.psum_scatter(
            grad_w_out.astype(jnp.bfloat16), "dp", scatter_dimension=1, tiled=True
        ).astype(jnp.float32),
    )
    (
        grad_b_query,
        grad_b_value,
        grad_b_inner,
        grad_b_out,
        grad_b_outer,
        grad_ln1_gain,
        grad_ln1_bias,
        grad_ln2_gain,
        grad_ln2_bias,
    ) = (
        lax.psum(grad_b_query.astype(jnp.bfloat16), "dp").astype(jnp.float32),
        lax.psum(grad_b_value.astype(jnp.bfloat16), "dp").astype(jnp.float32),
        lax.psum(grad_b_inner.astype(jnp.bfloat16), "dp").astype(jnp.float32),
        lax.psum(grad_b_out.astype(jnp.bfloat16), "dp").astype(jnp.float32),
        lax.psum(grad_b_outer.astype(jnp.bfloat16), "dp").astype(jnp.float32),
        lax.psum(grad_ln1_gain.astype(jnp.bfloat16), "dp").astype(jnp.float32),
        lax.psum(grad_ln1_bias.astype(jnp.bfloat16), "dp").astype(jnp.float32),
        lax.psum(grad_ln2_gain.astype(jnp.bfloat16), "dp").astype(jnp.float32),
        lax.psum(grad_ln2_bias.astype(jnp.bfloat16), "dp").astype(jnp.float32),
    )
    return (
        output,
        grad_tokens,
        grad_w_query,
        grad_w_key,
        grad_w_value,
        grad_b_query,
        grad_b_value,
        grad_w_out,
        grad_b_out,
        grad_ln1_gain,
        grad_ln1_bias,
        grad_w_inner,
        grad_b_inner,
        grad_w_outer,
        grad_b_outer,
        grad_ln2_gain,
        grad_ln2_bias,
    )


def solution(mesh):
    return jax.shard_map(
        on_device,
        mesh=mesh,
        in_specs=(
            P("dp", None),
            P("dp", None),
            P(),
            P(),
            P("dp", "tensor"),
            P("dp", "tensor"),
            P("dp", "tensor"),
            P("tensor"),
            P("tensor"),
            P("tensor", "dp"),
            P(),
            P(),
            P(),
            P("dp", "tensor"),
            P("tensor"),
            P("tensor", "dp"),
            P(),
            P(),
            P(),
        ),
        out_specs=(
            P("dp", None),
            P("dp", None),
            P("dp", "tensor"),
            P("dp", "tensor"),
            P("dp", "tensor"),
            P("tensor"),
            P("tensor"),
            P("tensor", "dp"),
            P(),
            P(),
            P(),
            P("dp", "tensor"),
            P("tensor"),
            P("tensor", "dp"),
            P(),
            P(),
            P(),
        ),
        check_vma=False,
    )
```

profile of v0, /device:TPU:0, one launch (start us, length us, event | category | flops | bytes accessed | tf_op | source)
XLA Modules:
  0.0 1807.7 jit_solution(10736105335624038911)
XLA Ops:
  14.7 27.4 %all-gather.9.cloned.1.call-done = bf16[2048,512]{1,0:T(8,128)(2,1)} async-done(((bf16[256,512]{1,0:T(8,128)(2,1)}), bf16[2048,512]{1,0:T(8,128)(2,1)}) %all-gather.9.cloned.1.call-update) | async-done | bytes 2097168 | tf_op jit(solution)/shard_map/all_gather | solution.py:80
  52.8 25.2 %all-gather.11.cloned.1.call-done = bf16[2048,512]{1,0:T(8,128)(2,1)} async-done(((bf16[256,512]{1,0:T(8,128)(2,1)}), bf16[2048,512]{1,0:T(8,128)(2,1)}) %all-gather.11.cloned.1.call-update) | async-done | bytes 2097168 | tf_op jit(solution)/shard_map/all_gather | solution.py:81
  90.7 26.6 %all-gather.7.cloned.1.call-done = bf16[2048,512]{1,0:T(8,128)(2,1)} async-done(((bf16[256,512]{1,0:T(8,128)(2,1)}), bf16[2048,512]{1,0:T(8,128)(2,1)}) %all-gather.7.cloned.1.call-update) | async-done | bytes 2097168 | tf_op jit(solution)/shard_map/all_gather | solution.py:79
  127.6 128.1 %while.31 = (s32[]{:T(128)}, bf16[2,512,4,128]{3,1,2,0:T(8,128)(2,1)}, f32[2,4,512,1]{2,1,3,0:T(4,128)S(1)}, bf16[2,512,4,128]{3,1,2,0:T(8,128)(2,1)}, s32[]{:T(...) while((s32[]{:T(128)}, ...), condition=%wide.region_5.6_spmd.clone.clone, body=%wide.region_2.5_spmd.clone.clone.sunk | while | flops 2204106752 | bytes 137967920 | solution.py:120
  164.7 14.5 select_select_fusion.6
  228.7 14.5 select_select_fusion.6
  271.7 169.3 %all-reduce.6.cloned.1.call-done = f32[1024,2048]{1,0:T(8,128)} async-done(((f32[1024,2048]{1,0:T(8,128)}), f32[1024,2048]{1,0:T(8,128)}) %all-reduce.6.cloned.1.call-update) | async-done | bytes 8388624 | tf_op jit(solution)/shard_map/psum | solution.py:32
  451.1 74.8 %all-gather.15.cloned.1.call-done = bf16[2048,2048]{1,0:T(8,128)(2,1)} async-done(((bf16[256,2048]{1,0:T(8,128)(2,1)}), bf16[2048,2048]{1,0:T(8,128)(2,1)}) %all-gather.15.cloned.1.call-update) | async-done | bytes 8388624 | tf_op jit(solution)/shard_map/all_gather | solution.py:128
  525.9 15.8 fusion.87
  541.7 67.5 %all-gather.17.cloned.1.call-done = bf16[2048,2048]{1,0:T(8,128)(2,1)} async-done(((bf16[2048,256]{1,0:T(8,128)(2,1)}), bf16[2048,2048]{1,0:T(8,128)(2,1)}) %all-gather.17.cloned.1.call-update) | async-done | bytes 8388624 | tf_op jit(solution)/shard_map/all_gather | solution.py:129
  609.2 17.3 fusion.85
  627.5 169.5 %all-reduce.8.cloned.1.call-done = f32[1024,2048]{1,0:T(8,128)} async-done(((f32[1024,2048]{1,0:T(8,128)}), f32[1024,2048]{1,0:T(8,128)}) %all-reduce.8.cloned.1.call-update) | async-done | bytes 8388624 | tf_op jit(solution)/shard_map/psum | solution.py:32
  818.5 23.4 %fusion.94 = (bf16[2048]{0:T(1024)(128)(2,1)}, bf16[1024,2048]{1,0:T(8,128)(2,1)}) fusion(bf16[2048,2048]{1,0:T(8,128)(2,1)} %all-gather.17.cloned.1.call-done, f32[1024,2048]{1,0:T(8,128)} %get-tuple-element.655, f32[1024]{0:T(1024)S(1)} %negate_multiply_fusion.1, f32[1024,2048]{1,0:T(8,128)} %fusion.87, f32[2048]{0:T(1024)S(1)} %copy-done.68), kind=kOutput, calls=%fused_computation.149 | convolution fusion | flops 8648652800 | bytes 29376512 | tf_op jit(solution)/shard_map/td,fd->tf/dot_general | solution.py:145
  842.0 14.5 fusion.95
  856.5 172.9 %all-reduce.10.cloned.1.call-done = f32[1024,2048]{1,0:T(8,128)} async-done(((f32[1024,2048]{1,0:T(8,128)}), f32[1024,2048]{1,0:T(8,128)}) %all-reduce.10.cloned.1.call-update) | async-done | bytes 8388624 | tf_op jit(solution)/shard_map/psum | solution.py:32
  1061.4 165.6 %while.32 = (s32[]{:T(128)}, f32[2048,4,128]{0,2,1:T(8,128)}, f32[2048,4,128]{0,2,1:T(8,128)}, bf16[2,512,4,128]{3,1,2,0:T(8,128)(2,1)}, bf16[2,512,4,128]{3,1,2...) while((s32[]{:T(128)}, f32[2048,4,128]{0,2,1:T(8,128)}, ...), condition=%wide.region_19.20_spmd.clone.clone.clone, body=%wide.region_17.19_spmd.clone.clone.clone.sunk | while | flops 5443420160 | bytes 367073888 | solution.py:204
  1082.1 14.4 select_select_fusion.7
  1249.2 47.1 %select_reduce_fusion.4 = (bf16[1024,512]{0,1:T(8,128)(2,1)}, bf16[1024,512]{0,1:T(8,128)(2,1)}, f32[1024,512]{0,1:T(8,128)S(1)}, f32[1024,512]{0,1:T(8,128)S(1)...) fusion(f32[2,1024,512]{1,0,2:T(2,128)} %reshape.188, pred[2]{0:T(512)(128)(4,1)S(1)} %copy-done.63, ...), kind=kLoop, calls=%fused_computation.97 | loop fusion | flops 9437184 | bytes 16777222 | tf_op jit(solution)/shard_map/reduce_sum | solution.py:213
  1334.2 15.4 convolution_convert_fusion.1
  1350.3 20.0 %convolution_convert_fusion = bf16[2048,2048]{1,0:T(8,128)(2,1)} fusion(f32[1024,2048]{1,0:T(8,128)} %get-tuple-element.655, f32[1024]{0:T(1024)S(1)} %copy-done.54, f32[1024,2048]{1,0:T(8,128)} %fusion.87, f32[2048]{0:T(1024)S(1)} %copy-done.69), kind=kOutput, calls=%fused_computation.84 | convolution fusion | flops 8619294720 | bytes 25178112 | tf_op jit(solution)/shard_map/tf,td->fd/dot_general | solution.py:144
  1403.1 88.7 %reduce-scatter.15.cloned.1.call-done = bf16[256,2048]{1,0:T(8,128)(2,1)} async-done(((bf16[2048,2048]{1,0:T(8,128)(2,1)}), bf16[256,2048]{1,0:T(8,128)(2,1)}) %reduce-scatter.15.cloned.1.call-update) | async-done | bytes 1048592 | tf_op jit(solution)/shard_map/reduce_scatter | solution.py:153
  1494.7 87.5 %reduce-scatter.17.cloned.1.call-done = bf16[2048,256]{1,0:T(8,128)(2,1)} async-done(((bf16[2048,2048]{1,0:T(8,128)(2,1)}), bf16[2048,256]{1,0:T(8,128)(2,1)}) %reduce-scatter.17.cloned.1.call-update) | async-done | bytes 1048592 | tf_op jit(solution)/shard_map/reduce_scatter | solution.py:156
  1584.9 172.1 %all-reduce.12.cloned.1.call-done = f32[1024,2048]{1,0:T(8,128)} async-done(((f32[1024,2048]{1,0:T(8,128)}), f32[1024,2048]{1,0:T(8,128)}) %all-reduce.12.cloned.1.call-update) | async-done | bytes 8388624 | tf_op jit(solution)/shard_map/psum | solution.py:32
  1767.0 28.6 %all-reduce = (bf16[512]{0:T(512)(128)(2,1)S(1)}, bf16[512]{0:T(512)(128)(2,1)S(1)}, bf16[2048]{0:T(1024)(128)(2,1)S(1)}, bf16[2048]{0:T(1024)(128)(2,1)S(1)}, b...) all-reduce(bf16[512]{0:T(512)(128)(2,1)S(1)} %bitcast.117, ...), channel_id=1, replica_groups=mesh['dp'=8,'tensor'=4] {'dp'}, use_global_device_ids=true, to_apply=%region_31.32 | all-reduce | flops 15360 | bytes 61440 | tf_op jit(solution)/shard_map/psum | solution.py:262
  (392 shorter events, 484.7 us)
Async XLA Ops:
  7.2 34.8 %all-gather.9.cloned.1.call-start = ((), (), s32[]{:S(2)}) async-start(), calls=%async_computation.7 | async-start | bytes 2359296 | tf_op jit(solution)/shard_map/all_gather | solution.py:80
  9.0 68.9 %all-gather.11.cloned.1.call-start = ((), (), s32[]{:S(2)}) async-start(), calls=%async_computation.8 | async-start | bytes 2359296 | tf_op jit(solution)/shard_map/all_gather | solution.py:81
  10.9 106.4 %all-gather.7.cloned.1.call-start = ((), (), s32[]{:S(2)}) async-start(), calls=%async_computation.6 | async-start | bytes 2359296 | tf_op jit(solution)/shard_map/all_gather | solution.py:79
  12.7 245.8 %all-gather.13.cloned.1.call-start = ((), (), s32[]{:S(2)}) async-start(), calls=%async_computation.9 | async-start | bytes 2359296 | tf_op jit(solution)/shard_map/all_gather | solution.py:82
  14.6 426.4 %all-reduce.6.cloned.1.call-start = ((), (), s32[]{:S(2)}) async-start(), calls=%async_computation.10 | async-start | bytes 16777216 | tf_op jit(solution)/shard_map/psum | solution.py:32
  47.3 79.2 %collective-permute-start.1 = (bf16[1024,512]{1,0:T(8,128)(2,1)S(1)}, bf16[1024,512]{1,0:T(8,128)(2,1)}, u32[]{:S(2)}, u32[]{:S(2)}) collective-permute-start(bf16[1024,512]{1,0:T(8,128)(2,1)S(1)} %convolution_convert_fusion.7), channel_id=1, source_target_pairs={{4,0},{8,4},{12,8},{16,12},{20,16},{24,20},{28,24},{5,1},{9,5},{13... | collective-permute-start | bytes 3145736 | tf_op jit(solution)/shard_map/ppermute | solution.py:14
  48.7 77.7 %collective-permute-start = (bf16[1024,512]{1,0:T(8,128)(2,1)S(1)}, bf16[1024,512]{1,0:T(8,128)(2,1)}, u32[]{:S(2)}, u32[]{:S(2)}) collective-permute-start(bf16[1024,512]{1,0:T(8,128)(2,1)S(1)} %convolution_convert_fusion.7), channel_id=1, source_target_pairs={{0,4},{4,8},{8,12},{12,16},{16,20},{20,24},{24,28},{1,5},{5,9},{9,... | collective-permute-start | bytes 3145736 | tf_op jit(solution)/shard_map/ppermute | solution.py:14
  83.2 43.3 %collective-permute-start.3 = (bf16[1024,512]{1,0:T(8,128)(2,1)S(1)}, bf16[1024,512]{1,0:T(8,128)(2,1)}, u32[]{:S(2)}, u32[]{:S(2)}) collective-permute-start(bf16[1024,512]{1,0:T(8,128)(2,1)S(1)} %add_convert_fusion.4), channel_id=1, source_target_pairs={{4,0},{8,4},{12,8},{16,12},{20,16},{24,20},{28,24},{5,1},{9,5},{13... | collective-permute-start | bytes 3145736 | tf_op jit(solution)/shard_map/ppermute | solution.py:14
  84.5 42.0 %collective-permute-start.2 = (bf16[1024,512]{1,0:T(8,128)(2,1)S(1)}, bf16[1024,512]{1,0:T(8,128)(2,1)}, u32[]{:S(2)}, u32[]{:S(2)}) collective-permute-start(bf16[1024,512]{1,0:T(8,128)(2,1)S(1)} %add_convert_fusion.4), channel_id=1, source_target_pairs={{0,4},{4,8},{8,12},{12,16},{16,20},{20,24},{24,28},{1,5},{5,9},{9,... | collective-permute-start | bytes 3145736 | tf_op jit(solution)/shard_map/ppermute | solution.py:14
  265.9 260.0 %all-gather.15.cloned.1.call-start = ((), (), s32[]{:S(2)}) async-start(), calls=%async_computation.11 | async-start | bytes 9437184 | tf_op jit(solution)/shard_map/all_gather | solution.py:128
  268.7 340.5 %all-gather.17.cloned.1.call-start = ((), (), s32[]{:S(2)}) async-start(), calls=%async_computation.12 | async-start | bytes 9437184 | tf_op jit(solution)/shard_map/all_gather | solution.py:129
  271.5 525.5 %all-reduce.8.cloned.1.call-start = ((), (), s32[]{:S(2)}) async-start(), calls=%async_computation.13 | async-start | bytes 16777216 | tf_op jit(solution)/shard_map/psum | solution.py:32
  626.6 402.8 %all-reduce.10.cloned.1.call-start = ((), (), s32[]{:S(2)}) async-start(), calls=%async_computation.14 | async-start | bytes 16777216 | tf_op jit(solution)/shard_map/psum | solution.py:32
  856.5 529.0 %reduce-scatter.13.cloned.1.call-start = ((), (), s32[]{:S(2)}) async-start(), calls=%async_computation.19 | async-start | bytes 2359296 | tf_op jit(solution)/shard_map/reduce_scatter | solution.py:247
  1060.2 327.1 %reduce-scatter.7.cloned.1.call-start = ((), (), s32[]{:S(2)}) async-start(), calls=%async_computation.16 | async-start | bytes 2359296 | tf_op jit(solution)/shard_map/reduce_scatter | solution.py:238
  1236.0 153.2 %reduce-scatter.11.cloned.1.call-start = ((), (), s32[]{:S(2)}) async-start(), calls=%async_computation.18 | async-start | bytes 2359296 | tf_op jit(solution)/shard_map/reduce_scatter | solution.py:244
  1296.3 4.6 collective-permute-start.7
  1297.6 5.5 collective-permute-start.6
  1307.3 94.0 %reduce-scatter.9.cloned.1.call-start = ((), (), s32[]{:S(2)}) async-start(), calls=%async_computation.17 | async-start | bytes 2359296 | tf_op jit(solution)/shard_map/reduce_scatter | solution.py:241
  1307.3 15.0 collective-permute-start.4
  1319.9 6.7 collective-permute-start.5
  1334.1 157.8 %reduce-scatter.15.cloned.1.call-start = ((), (), s32[]{:S(2)}) async-start(), calls=%async_computation.20 | async-start | bytes 9437184 | tf_op jit(solution)/shard_map/reduce_scatter | solution.py:153
  1349.6 232.5 %reduce-scatter.17.cloned.1.call-start = ((), (), s32[]{:S(2)}) async-start(), calls=%async_computation.21 | async-start | bytes 9437184 | tf_op jit(solution)/shard_map/reduce_scatter | solution.py:156
  1370.3 386.7 %all-reduce.12.cloned.1.call-start = ((), (), s32[]{:S(2)}) async-start(), calls=%async_computation.15 | async-start | bytes 16777216 | tf_op jit(solution)/shard_map/psum | solution.py:32
  (93 other events, 4401.2 us)
Sparse Core Ops, SparseCore 0:
  10.2 31.7 all-gather.8
  44.2 33.7 all-gather.10
  80.1 37.1 all-gather.6
  119.3 33.6 all-gather.12
  266.0 174.9 all-reduce.5
  443.1 82.7 all-gather.14
  528.1 81.0 all-gather.16
  626.7 170.2 all-reduce.7
  856.6 172.7 all-reduce.9
  1060.3 36.5 reduce-scatter.12
  1236.1 36.5 reduce-scatter.6
  1307.4 52.8 reduce-scatter.10
  1363.2 37.9 reduce-scatter.8
  1403.5 88.3 reduce-scatter.14
  1494.1 87.9 reduce-scatter.16
  1586.5 170.4 all-reduce.11
where the time goes:
time: 1810 us
  waiting for transfers between devices  1100 us (61%)
  matrix products  235 us (13%)
  other arithmetic  222 us (12%)
  local copies, waits for them, and re-layouts  176 us (10%)
  starting transfers between devices  30.5 us (2%)
  blocking collectives  28.6 us (2%)
    psum x4, waiting for transfers between devices, tensor_total(): return lax.psum(part, 'tensor')  684 us
    reduce_scatter x1, waiting for transfers between devices, on_device(): lax.psum_scatter(grad_w_inner.astype(jnp.bfloat16), 'dp', scatter_dimensi...  88.7 us
    reduce_scatter x1, waiting for transfers between devices, on_device(): lax.psum_scatter(grad_w_outer.astype(jnp.bfloat16), 'dp', scatter_dimensi...  87.5 us
    all_gather x1, waiting for transfers between devices, on_device(): lax.all_gather(w_inner.astype(jnp.bfloat16), 'dp', axis=0, tiled=True)  74.8 us
    all_gather x1, waiting for transfers between devices, on_device(): lax.all_gather(w_outer.astype(jnp.bfloat16), 'dp', axis=1, tiled=True)  67.5 us
    select_n x4, other arithmetic, on_device(): key_slab = jnp.where(far_hit, far_key[None], key_slab)  57.8 us
    dot_general x6, matrix products, mat_bf(): return jnp.dot(left, right, preferred_element_type=jnp.float32)  57 us
    reduce_sum x1, other arithmetic, on_device(): send_key = jnp.sum(jnp.where(far_hit, key_grad_slab, 0.0), axis=0)  47.1 us
  transfers between devices with their start and end apart: 24, of which 15 were waited for; matrix products, arithmetic and copies ran while one was open for 26% of the time, Pallas kernels for 0%

commit v1 on v0

--- a/solution.py
+++ b/solution.py
@@ -1,3 +1,4 @@
+import functools
 import jax
 import jax.numpy as jnp
 from jax import lax
@@ -8,6 +9,13 @@
 norm_eps = 1e-12
 
 
+def tell_tracks_on_mesh(view, axis_name):
+    return lax.all_gather(view, axis_name).sum(axis=0)
+
+
+_show_tables = functools.partial(tell_tracks_on_mesh, axis_name="tensor")
+
+
 def passed_along(value, axis, steps):
     count = lax.axis_size(axis)
     leading, last = (max(0, -steps), min(count, count - steps))
@@ -29,7 +37,7 @@
 
 
 def tensor_total(part):
-    return lax.psum(part, "tensor")
+    return _show_tables(part)
 
 
 def on_device(

time: 1810 us -> 2240 us (1.24)
  waiting for transfers between devices: 1100 us -> 1400 us
  other arithmetic: 222 us -> 288 us
  matrix products: 235 us -> 271 us
  local copies, waits for them, and re-layouts: 176 us -> 200 us
    all_gather x0 -> x4, waiting for transfers between devices: none -> 1150 us  [tell_tracks_on_mesh(): return lax.all_gather(view, axis_name).sum(axis=0)]
    psum x4 -> x0, waiting for transfers between devices: 684 us -> none  [tensor_total(): return lax.psum(part, 'tensor')]
    reduce_scatter x1, waiting for transfers between devices: 88.7 us -> 0.01 us  [on_device(): lax.psum_scatter(grad_w_inner.astype(jnp.bfloat16), 'dp', scatter_dimensi...]
    reduce_scatter x1, waiting for transfers between devices: 87.5 us -> 0.02 us  [on_device(): lax.psum_scatter(grad_w_outer.astype(jnp.bfloat16), 'dp', scatter_dimensi...]
    reduce_sum x0 -> x4, other arithmetic: none -> 66.4 us  [tell_tracks_on_mesh(): return lax.all_gather(view, axis_name).sum(axis=0)]
    reduce_scatter x1, waiting for transfers between devices: 10.2 us -> 38.7 us  [on_device(): lax.psum_scatter(grad_w_key.astype(jnp.bfloat16), 'dp', scatter_dimension...]
  transfers between devices with their start and end apart: 24 -> 24, of which waited for: 15 -> 15; matrix products, arithmetic and copies ran while one was open for 26% -> 27% of each run, Pallas kernels for 0% -> 0%
where the time goes in v1:
time: 2240 us; the launch traced here: 2230 us
  waiting for transfers between devices  1400 us (62%)
  other arithmetic  288 us (13%)
  matrix products  271 us (12%)
  local copies, waits for them, and re-layouts  200 us (9%)
  blocking collectives  28.6 us (1%)
  starting transfers between devices  27.3 us (1%)
    all_gather x4, waiting for transfers between devices, tell_tracks_on_mesh(): return lax.all_gather(view, axis_name).sum(axis=0)  1150 us
    all_gather x1, waiting for transfers between devices, on_device(): lax.all_gather(w_outer.astype(jnp.bfloat16), 'dp', axis=1, tiled=True)  67.4 us
    reduce_sum x4, other arithmetic, tell_tracks_on_mesh(): return lax.all_gather(view, axis_name).sum(axis=0)  66.4 us
    select_n x4, other arithmetic, on_device(): key_slab = jnp.where(far_hit, far_key[None], key_slab)  57.7 us
    dot_general x6, matrix products, mat_bf(): return jnp.dot(left, right, preferred_element_type=jnp.float32)  57.3 us
    all_gather x1, waiting for transfers between devices, on_device(): lax.all_gather(w_inner.astype(jnp.bfloat16), 'dp', axis=0, tiled=True)  56.1 us
    broadcast_in_dim x16, local copies, waits for them, and re-layouts, on_device(): value_slab = jnp.where(far_hit, far_value[None], value_slab)  53.3 us
    reduce_sum x1, other arithmetic, on_device(): send_key = jnp.sum(jnp.where(far_hit, key_grad_slab, 0.0), axis=0)  47 us
  transfers between devices with their start and end apart: 24, of which 15 were waited for; matrix products, arithmetic and copies ran while one was open for 27% of the time, Pallas kernels for 0%

profile of v1, /device:TPU:0, one launch (start us, length us, event | category | flops | bytes accessed | tf_op | source)
XLA Modules:
  0.0 2230.5 jit_solution(3793240282463763023)
XLA Ops:
  14.7 27.4 %all-gather.17.cloned.1.call-done = bf16[2048,512]{1,0:T(8,128)(2,1)} async-done(((bf16[256,512]{1,0:T(8,128)(2,1)}), bf16[2048,512]{1,0:T(8,128)(2,1)}) %all-gather.17.cloned.1.call-update) | async-done | bytes 2097168 | tf_op jit(solution)/shard_map/all_gather | solution.py:88
  50.9 26.9 %all-gather.19.cloned.1.call-done = bf16[2048,512]{1,0:T(8,128)(2,1)} async-done(((bf16[256,512]{1,0:T(8,128)(2,1)}), bf16[2048,512]{1,0:T(8,128)(2,1)}) %all-gather.19.cloned.1.call-update) | async-done | bytes 2097168 | tf_op jit(solution)/shard_map/all_gather | solution.py:89
  89.8 27.3 %all-gather.15.cloned.1.call-done = bf16[2048,512]{1,0:T(8,128)(2,1)} async-done(((bf16[256,512]{1,0:T(8,128)(2,1)}), bf16[2048,512]{1,0:T(8,128)(2,1)}) %all-gather.15.cloned.1.call-update) | async-done | bytes 2097168 | tf_op jit(solution)/shard_map/all_gather | solution.py:87
  129.3 128.8 %while.31 = (s32[]{:T(128)}, bf16[2,512,4,128]{3,1,2,0:T(8,128)(2,1)}, f32[2,4,512,1]{2,1,3,0:T(4,128)S(1)}, bf16[2,512,4,128]{3,1,2,0:T(8,128)(2,1)}, s32[]{:T(...) while((s32[]{:T(128)}, ...), condition=%wide.region_5.6_spmd.clone.clone, body=%wide.region_2.5_spmd.clone.clone.sunk | while | flops 2204106752 | bytes 137968432 | solution.py:128
  275.4 294.7 %all-gather.27.cloned.1.call-done = f32[4096,2048]{1,0:T(8,128)} async-done(((f32[1024,2048]{1,0:T(8,128)}), f32[4096,2048]{1,0:T(8,128)}) %all-gather.27.cloned.1.call-update) | async-done | bytes 33554448 | tf_op jit(solution)/shard_map/all_gather | solution.py:13
  570.0 17.3 reduce_sum.324
  598.1 56.1 %all-gather.23.cloned.1.call-done = bf16[2048,2048]{1,0:T(8,128)(2,1)} async-done(((bf16[256,2048]{1,0:T(8,128)(2,1)}), bf16[2048,2048]{1,0:T(8,128)(2,1)}) %all-gather.23.cloned.1.call-update) | async-done | bytes 8388624 | tf_op jit(solution)/shard_map/all_gather | solution.py:136
  654.2 15.8 fusion.87
  670.0 67.4 %all-gather.25.cloned.1.call-done = bf16[2048,2048]{1,0:T(8,128)(2,1)} async-done(((bf16[2048,256]{1,0:T(8,128)(2,1)}), bf16[2048,2048]{1,0:T(8,128)(2,1)}) %all-gather.25.cloned.1.call-update) | async-done | bytes 8388624 | tf_op jit(solution)/shard_map/all_gather | solution.py:137
  737.4 17.3 fusion.85
  755.4 294.8 %all-gather.29.cloned.1.call-done = f32[4096,2048]{1,0:T(8,128)} async-done(((f32[1024,2048]{1,0:T(8,128)}), f32[4096,2048]{1,0:T(8,128)}) %all-gather.29.cloned.1.call-update) | async-done | bytes 33554448 | tf_op jit(solution)/shard_map/all_gather | solution.py:13
  1050.3 16.3 reduce_sum.327
  1088.2 23.6 %fusion.94 = (bf16[2048]{0:T(1024)(128)(2,1)}, bf16[1024,2048]{1,0:T(8,128)(2,1)}) fusion(bf16[2048,2048]{1,0:T(8,128)(2,1)} %all-gather.25.cloned.1.call-done, f32[1024,2048]{1,0:T(8,128)} %get-tuple-element.655, f32[1024]{0:T(1024)S(1)} %negate_multiply_fusion.1, f32[1024,2048]{1,0:T(8,128)} %fusion.87, f32[2048]{0:T(1024)S(1)} %copy-done.57), kind=kOutput, calls=%fused_computation.149 | convolution fusion | flops 8648652800 | bytes 29376512 | tf_op jit(solution)/shard_map/td,fd->tf/dot_general | solution.py:153
  1111.8 14.5 fusion.95
  1126.4 20.8 convolution_convert_fusion
  1147.3 16.6 convolution_convert_fusion.1
  1163.9 259.8 %all-gather.31.cloned.1.call-done = f32[4096,2048]{1,0:T(8,128)} async-done(((f32[1024,2048]{1,0:T(8,128)}), f32[4096,2048]{1,0:T(8,128)}) %all-gather.31.cloned.1.call-update) | async-done | bytes 33554448 | tf_op jit(solution)/shard_map/all_gather | solution.py:13
  1423.7 16.8 reduce_sum.332
  1475.0 217.7 %while.32 = (s32[]{:T(128)}, f32[2048,4,128]{0,2,1:T(8,128)}, f32[2048,4,128]{0,2,1:T(8,128)}, bf16[2,512,4,128]{3,1,2,0:T(8,128)(2,1)}, bf16[2,512,4,128]{3,1,2...) while((s32[]{:T(128)}, f32[2048,4,128]{0,2,1:T(8,128)}, ...), condition=%wide.region_19.20_spmd.clone.clone.clone, body=%wide.region_17.19_spmd.clone.clone.clone.sunk | while | flops 5443420160 | bytes 264313680 | solution.py:212
  1715.1 47.0 %select_reduce_fusion.4 = (bf16[1024,512]{0,1:T(8,128)(2,1)}, bf16[1024,512]{0,1:T(8,128)(2,1)}, f32[1024,512]{0,1:T(8,128)S(1)}, f32[1024,512]{0,1:T(8,128)S(1)...) fusion(f32[2,1024,512]{1,0,2:T(2,128)} %reshape.188, pred[2]{0:T(512)(128)(4,1)S(1)} %copy-done.51, ...), kind=kLoop, calls=%fused_computation.97 | loop fusion | flops 9437184 | bytes 16777222 | tf_op jit(solution)/shard_map/reduce_sum | solution.py:221
  1827.2 38.7 %reduce-scatter.9.cloned.1.call-done = bf16[256,512]{0,1:T(8,128)(2,1)} async-done(((bf16[2048,512]{0,1:T(8,128)(2,1)}), bf16[256,512]{0,1:T(8,128)(2,1)}) %reduce-scatter.9.cloned.1.call-update) | async-done | bytes 262160 | tf_op jit(solution)/shard_map/reduce_scatter | solution.py:249
  1867.8 295.8 %all-gather.33.cloned.1.call-done = f32[4096,2048]{1,0:T(8,128)} async-done(((f32[1024,2048]{1,0:T(8,128)}), f32[4096,2048]{1,0:T(8,128)}) %all-gather.33.cloned.1.call-update) | async-done | bytes 33554448 | tf_op jit(solution)/shard_map/all_gather | solution.py:13
  2163.6 16.0 reduce_sum.341
  2189.7 28.6 %all-reduce = (bf16[512]{0:T(512)(128)(2,1)S(1)}, bf16[512]{0:T(512)(128)(2,1)S(1)}, bf16[2048]{0:T(1024)(128)(2,1)S(1)}, bf16[2048]{0:T(1024)(128)(2,1)S(1)}, b...) all-reduce(bf16[512]{0:T(512)(128)(2,1)S(1)} %bitcast.125, ...), channel_id=1, replica_groups=mesh['dp'=8,'tensor'=4] {'dp'}, use_global_device_ids=true, to_apply=%region_31.32 | all-reduce | flops 15360 | bytes 61440 | tf_op jit(solution)/shard_map/psum | solution.py:270
  (354 shorter events, 575.1 us)
Async XLA Ops:
  7.2 34.8 %all-gather.17.cloned.1.call-start = ((), (), s32[]{:S(2)}) async-start(), calls=%async_computation.7 | async-start | bytes 2359296 | tf_op jit(solution)/shard_map/all_gather | solution.py:88
  9.0 68.8 %all-gather.19.cloned.1.call-start = ((), (), s32[]{:S(2)}) async-start(), calls=%async_computation.8 | async-start | bytes 2359296 | tf_op jit(solution)/shard_map/all_gather | solution.py:89
  10.9 106.2 %all-gather.15.cloned.1.call-start = ((), (), s32[]{:S(2)}) async-start(), calls=%async_computation.6 | async-start | bytes 2359296 | tf_op jit(solution)/shard_map/all_gather | solution.py:87
  12.7 249.3 %all-gather.21.cloned.1.call-start = ((), (), s32[]{:S(2)}) async-start(), calls=%async_computation.9 | async-start | bytes 2359296 | tf_op jit(solution)/shard_map/all_gather | solution.py:90
  14.6 555.4 %all-gather.27.cloned.1.call-start = ((), (), s32[]{:S(2)}) async-start(), calls=%async_computation.18 | async-start | bytes 41943040 | tf_op jit(solution)/shard_map/all_gather | solution.py:13
  47.3 80.9 %collective-permute-start = (bf16[1024,512]{1,0:T(8,128)(2,1)S(1)}, bf16[1024,512]{1,0:T(8,128)(2,1)S(1)}, u32[]{:S(2)}, u32[]{:S(2)}) collective-permute-start(bf16[1024,512]{1,0:T(8,128)(2,1)S(1)} %convolution_convert_fusion.7), channel_id=1, source_target_pairs={{0,4},{4,8},{8,12},{12,16},{16,20},{20,24},{24,28},{1,5},{5,9},{9,... | collective-permute-start | bytes 3145736 | tf_op jit(solution)/shard_map/ppermute | solution.py:22
  49.6 78.6 %collective-permute-start.1 = (bf16[1024,512]{1,0:T(8,128)(2,1)S(1)}, bf16[1024,512]{1,0:T(8,128)(2,1)}, u32[]{:S(2)}, u32[]{:S(2)}) collective-permute-start(bf16[1024,512]{1,0:T(8,128)(2,1)S(1)} %convolution_convert_fusion.7), channel_id=1, source_target_pairs={{4,0},{8,4},{12,8},{16,12},{20,16},{24,20},{28,24},{5,1},{9,5},{13... | collective-permute-start | bytes 3145736 | tf_op jit(solution)/shard_map/ppermute | solution.py:22
  83.1 45.2 %collective-permute-start.2 = (bf16[1024,512]{1,0:T(8,128)(2,1)S(1)}, bf16[1024,512]{1,0:T(8,128)(2,1)}, u32[]{:S(2)}, u32[]{:S(2)}) collective-permute-start(bf16[1024,512]{1,0:T(8,128)(2,1)S(1)} %add_convert_fusion.4), channel_id=1, source_target_pairs={{0,4},{4,8},{8,12},{12,16},{16,20},{20,24},{24,28},{1,5},{5,9},{9,... | collective-permute-start | bytes 3145736 | tf_op jit(solution)/shard_map/ppermute | solution.py:22
  86.2 42.0 %collective-permute-start.3 = (bf16[1024,512]{1,0:T(8,128)(2,1)S(1)}, bf16[1024,512]{1,0:T(8,128)(2,1)}, u32[]{:S(2)}, u32[]{:S(2)}) collective-permute-start(bf16[1024,512]{1,0:T(8,128)(2,1)S(1)} %add_convert_fusion.4), channel_id=1, source_target_pairs={{4,0},{8,4},{12,8},{16,12},{20,16},{24,20},{28,24},{5,1},{9,5},{13... | collective-permute-start | bytes 3145736 | tf_op jit(solution)/shard_map/ppermute | solution.py:22
  269.8 384.4 %all-gather.23.cloned.1.call-start = ((), (), s32[]{:S(2)}) async-start(), calls=%async_computation.10 | async-start | bytes 9437184 | tf_op jit(solution)/shard_map/all_gather | solution.py:136
  272.6 464.8 %all-gather.25.cloned.1.call-start = ((), (), s32[]{:S(2)}) async-start(), calls=%async_computation.11 | async-start | bytes 9437184 | tf_op jit(solution)/shard_map/all_gather | solution.py:137
  275.3 774.9 %all-gather.29.cloned.1.call-start = ((), (), s32[]{:S(2)}) async-start(), calls=%async_computation.19 | async-start | bytes 41943040 | tf_op jit(solution)/shard_map/all_gather | solution.py:13
  754.7 669.0 %all-gather.31.cloned.1.call-start = ((), (), s32[]{:S(2)}) async-start(), calls=%async_computation.20 | async-start | bytes 41943040 | tf_op jit(solution)/shard_map/all_gather | solution.py:13
  1126.3 686.5 %reduce-scatter.17.cloned.1.call-start = ((), (), s32[]{:S(2)}) async-start(), calls=%async_computation.17 | async-start | bytes 9437184 | tf_op jit(solution)/shard_map/reduce_scatter | solution.py:164
  1147.2 668.4 %reduce-scatter.15.cloned.1.call-start = ((), (), s32[]{:S(2)}) async-start(), calls=%async_computation.16 | async-start | bytes 9437184 | tf_op jit(solution)/shard_map/reduce_scatter | solution.py:161
  1163.8 655.9 %reduce-scatter.13.cloned.1.call-start = ((), (), s32[]{:S(2)}) async-start(), calls=%async_computation.15 | async-start | bytes 2359296 | tf_op jit(solution)/shard_map/reduce_scatter | solution.py:255
  1473.8 347.8 %reduce-scatter.7.cloned.1.call-start = ((), (), s32[]{:S(2)}) async-start(), calls=%async_computation.12 | async-start | bytes 2359296 | tf_op jit(solution)/shard_map/reduce_scatter | solution.py:246
  1701.7 123.7 %reduce-scatter.11.cloned.1.call-start = ((), (), s32[]{:S(2)}) async-start(), calls=%async_computation.14 | async-start | bytes 2359296 | tf_op jit(solution)/shard_map/reduce_scatter | solution.py:252
  1762.1 4.0 collective-permute-start.6
  1763.8 6.0 collective-permute-start.7
  1774.0 91.9 %reduce-scatter.9.cloned.1.call-start = ((), (), s32[]{:S(2)}) async-start(), calls=%async_computation.13 | async-start | bytes 2359296 | tf_op jit(solution)/shard_map/reduce_scatter | solution.py:249
  1774.1 16.5 collective-permute-start.4
  1788.1 4.8 collective-permute-start.5
  1800.4 363.2 %all-gather.33.cloned.1.call-start = ((), (), s32[]{:S(2)}) async-start(), calls=%async_computation.21 | async-start | bytes 41943040 | tf_op jit(solution)/shard_map/all_gather | solution.py:13
  (72 other events, 1680.4 us)
Sparse Core Ops, SparseCore 0:
  10.2 31.7 all-gather.16
  44.2 33.6 all-gather.18
  80.0 37.0 all-gather.14
  119.1 33.7 all-gather.20
  269.9 300.1 all-gather.26
  572.1 82.0 all-gather.22
  656.3 81.0 all-gather.24
  754.8 295.3 all-gather.28
  1126.4 297.1 all-gather.30
  1425.8 89.5 reduce-scatter.16
  1517.8 87.9 reduce-scatter.14
  1607.9 34.1 reduce-scatter.12
  1701.8 35.6 reduce-scatter.6
  1774.1 51.1 reduce-scatter.10
  1827.5 38.4 reduce-scatter.8
  1867.6 295.9 all-gather.32
